TPU v7x, 32 devices: a whole 2x2x4 slice. The times are simulated.
32 devices in a mesh: groups: 2 (over y), frames: 16 (over z, x, core).
Axes of the slice: x: 2, y: 2, z: 4, core: 2. Of those that a mesh axis runs over, the one named last changes fastest.
Arguments:
- video_frames: bfloat16 [64, 1024, 1024], P(('groups', 'frames')), parts along dimension 0, may hold values from -6 to 6
- segments: int32 [64], P('groups'), parts along dimension 0, may hold values from 0 to 3, never falling along the last dimension, each value on 1 to 29 neighbouring positions
- ref_pick: int32 [8], P('groups'), parts along dimension 0, may hold values from 0 to 4095
- band_taps: bfloat16 [32], replicated, may hold values from -2 to 2
Outputs:
- motion: float32 [64, 256, 256], P(('groups', 'frames')), parts along dimension 0
There are 2 independent parts, one for each index of `groups`. A program takes and returns all parts, laid end to end along the dimension named above; an argument that names none is the same for every part. Nothing has to cross between parts.
Inputs may be any that keep to these rules, and one draw needn't show every extreme that they name: Segment numbers never fall along the frames; each of the 4 segments holds 1 to 29 frames and one holds exactly 29.
All inputs are finite; a program needn't handle non-finite values.
Results may differ from a plain program's by a relative error of at most 0.012.
Values may be sent and summed in bfloat16 or wider, within the bound.
A program may use at most 128 MiB of HBM per device.

v0:
```python
import math

import jax
import jax.numpy as jnp
from jax import lax
from jax.sharding import PartitionSpec as P

IMG = 1024
ORIENT = 4
NSEG = 4
QUART = 256


blur_sigma = 2.0
gabor_sigma = 2.0
wave_number = math.pi / 2.0
gabor_gain = 2.0


def spread(x, axis, root):
    mine = lax.axis_index(axis) == root
    return lax.psum(jnp.where(mine, x, jnp.zeros_like(x)), axis)


def make_down(full_size, quarter):
    position = jnp.arange(quarter, dtype=jnp.float32)[:, None]
    columns = jnp.arange(full_size, dtype=jnp.float32)[None, :]
    offset_grid = columns - 4.0 * position - 1.5
    weight = jnp.exp(-offset_grid * offset_grid / (2.0 * blur_sigma * blur_sigma))
    return (weight / jnp.sum(weight, axis=1, keepdims=True)).astype(jnp.bfloat16)


def gabor_tables(quarter, orient):
    position = jnp.arange(quarter, dtype=jnp.float32)
    offset_grid = position[None, :] - position[:, None]
    envelope = gabor_gain * jnp.exp(-offset_grid * offset_grid / (2.0 * gabor_sigma * gabor_sigma))
    angles = jnp.arange(orient, dtype=jnp.float32) * (math.pi / orient)
    wave_x = wave_number * jnp.cos(angles)
    wave_y = wave_number * jnp.sin(angles)
    phase_y = wave_y[:, None, None] * offset_grid[None]
    left_table = jnp.stack([envelope * jnp.cos(phase_y), envelope * jnp.sin(phase_y)], axis=2)
    left_table = left_table.reshape(orient * quarter * 2, quarter).astype(jnp.bfloat16)
    phase_x = wave_x[:, None, None] * (-offset_grid)[None]
    real_part = envelope * jnp.cos(phase_x)
    imag_part = envelope * jnp.sin(phase_x)
    upper_half = jnp.concatenate([real_part, imag_part], axis=2)
    lower_half = jnp.concatenate([-imag_part, real_part], axis=2)
    right_table = jnp.concatenate([upper_half, lower_half], axis=1).astype(jnp.bfloat16)
    return (left_table, right_table)


def phase_terms(coeffs, per_frame):
    quarter = coeffs.shape[-1] // 2
    coeff_real = coeffs[..., :quarter].astype(jnp.float32)
    coeff_imag = coeffs[..., quarter:].astype(jnp.float32)
    ref_real = per_frame[..., :quarter].astype(jnp.float32)
    ref_imag = per_frame[..., quarter:].astype(jnp.float32)
    prod_real = coeff_real * ref_real + coeff_imag * ref_imag
    prod_imag = coeff_imag * ref_real - coeff_real * ref_imag
    phase_signal = (
        prod_imag / jnp.sqrt(prod_real * prod_real + prod_imag * prod_imag + 1.0)
    ).astype(jnp.bfloat16)
    amplitude = coeff_real * coeff_real + coeff_imag * coeff_imag
    return (phase_signal, amplitude)


def taps_matrix(band_taps, frame_count):
    frame_index = jnp.arange(frame_count, dtype=jnp.int32)
    lag_grid = frame_index[:, None] - frame_index[None, :]
    one_hot = (
        lag_grid[:, :, None] == jnp.arange(band_taps.shape[0], dtype=jnp.int32)[None, None, :]
    ).astype(jnp.float32)
    return jnp.einsum("tsk,k->ts", one_hot, band_taps.astype(jnp.float32)).astype(jnp.bfloat16)


def segment_refs(segments, ref_pick, segment_count):
    numbers = jnp.arange(segment_count, dtype=jnp.int32)
    starts = jnp.sum((segments[None, :] < numbers[:, None]).astype(jnp.int32), axis=1)
    counts = jnp.sum((segments[None, :] == numbers[:, None]).astype(jnp.int32), axis=1)
    return starts + ref_pick % counts


def body(video_frames, segments, ref_pick, band_taps):
    frames_here = video_frames.shape[0]
    down_matrix = make_down(IMG, QUART)
    left_table, right_table = gabor_tables(QUART, ORIENT)

    def reduce_frames(pictures):
        half_done = jnp.einsum(
            "nia,qa->niq", pictures, down_matrix, preferred_element_type=jnp.float32
        ).astype(jnp.bfloat16)
        return jnp.einsum(
            "qi,nik->nqk", down_matrix, half_done, preferred_element_type=jnp.float32
        ).astype(jnp.bfloat16)

    def filter_frames(reduced):
        stacked = jnp.einsum(
            "ra,nak->nrk", left_table, reduced, preferred_element_type=jnp.float32
        ).astype(jnp.bfloat16)
        stacked = stacked.reshape(reduced.shape[0], ORIENT, QUART, 2 * QUART)
        return jnp.einsum(
            "noya,oab->noyb", stacked, right_table, preferred_element_type=jnp.float32
        ).astype(jnp.bfloat16)

    small_own = reduce_frames(video_frames)
    coeff_own = filter_frames(small_own)
    ref_frames = segment_refs(segments, ref_pick, NSEG)
    gathered = []
    for segment in range(NSEG):
        root_index = ref_frames[segment] // frames_here
        local_index = ref_frames[segment] % frames_here
        payload = lax.dynamic_index_in_dim(video_frames, local_index, 0, keepdims=False)
        gathered.append(spread(payload, "frames", root_index))
    ref_coeff = filter_frames(reduce_frames(jnp.stack(gathered)))
    first_frame = lax.axis_index("frames") * frames_here
    own_ids = lax.dynamic_slice_in_dim(segments, first_frame, frames_here)
    select = (own_ids[:, None] == jnp.arange(NSEG, dtype=jnp.int32)[None, :]).astype(jnp.bfloat16)
    per_frame = jnp.dot(select, ref_coeff.reshape(NSEG, -1), preferred_element_type=jnp.float32)
    per_frame = per_frame.astype(jnp.bfloat16).reshape(coeff_own.shape)
    phase_signal, amplitude = phase_terms(coeff_own, per_frame)
    phase_signal = phase_signal.reshape(frames_here, ORIENT, QUART * QUART)
    pixel_rows = lax.all_to_all(phase_signal, "frames", split_axis=2, concat_axis=0, tiled=True)
    matrix = taps_matrix(band_taps, pixel_rows.shape[0])
    filtered = jnp.einsum(
        "ts,sop->top", matrix, pixel_rows, preferred_element_type=jnp.float32
    ).astype(jnp.bfloat16)
    filtered = lax.all_to_all(filtered, "frames", split_axis=0, concat_axis=2, tiled=True)
    filtered = filtered.reshape(frames_here, ORIENT, QUART, QUART).astype(jnp.float32)
    return jnp.sum(amplitude * filtered, axis=1) / (jnp.sum(amplitude, axis=1) + 1.0)


def solution(mesh):
    in_specs = (P(("groups", "frames"), None, None), P("groups"), P("groups"), P())
    out_specs = P(("groups", "frames"), None, None)
    return jax.shard_map(body, mesh=mesh, in_specs=in_specs, out_specs=out_specs, check_vma=False)
```

profile of v0, /device:TPU:1, one launch (start us, length us, event | category | flops | bytes accessed | tf_op | source)
XLA Modules:
  0.0 566.1 jit_solution(13110791398909881143)
XLA Ops:
  18.7 6.8 %dynamic-slice_select_fusion.3 = (bf16[1,1024,1024]{2,1,0:T(8,128)(2,1)}, bf16[1,1024,1024]{2,1,0:T(8,128)(2,1)}, bf16[1,1024,1024]{2,1,0:T(8,128)(2,1)}, bf16[1,1024,1024]{2,1,0:T(8,128)(2,1)}) fusion(bf16[2,1024,1024]{2,1,0:T(8,128)(2,1)} %param.4, s32[]{:T(128)S(6)} %select_n.101, pred[]{:T(512)S(6)} %eq.64, s32[]{:T(128)S(6)} %select_n.107, pred[]{:T(512)S(6)} %eq.65, ...), kind=kLoop, calls=%fused_computation.41 | loop fusion | flops 4194304 | bytes 16777236 | tf_op jit(solution)/shard_map/jit(_where)/select_n | solution.py:22
  25.9 4.2 fusion.52
  33.1 4.5 fusion.33
  37.6 3.0 fusion.10
  40.6 2.9 copy.77
  45.8 5.2 fusion.49
  53.8 144.2 %all-reduce.3.cloned.1.call-done = (bf16[1,1024,1024]{2,1,0:T(8,128)(2,1)}, bf16[1,1024,1024]{2,1,0:T(8,128)(2,1)}, bf16[1,1024,1024]{2,1,0:T(8,128)(2,1)}, bf16[1,1024,1024]{2,1,0:T(8,128)(2,1)}) async-done(((bf16[1,1024,1024]{2,1,0:T(8,128)(2,1)}, bf16[1,1024,1024]{2,1,0:T(8,128)(2,1)}, bf16[1,1024,1024]{2,1,0:T(8,128)(2,1)}, bf16[1,1024,1024]{2,1,0:T(8,128)(2,1)}), (bf16[1,1024,1024]{2,1,0:T(8,128)(2,1)}, ...) | async-done | bytes 8388624 | tf_op jit(solution)/shard_map/psum | solution.py:22
  198.0 8.3 %fusion.39 = bf16[4,256,256]{1,2,0:T(8,128)(2,1)} fusion(bf16[1,1024,1024]{2,1,0:T(8,128)(2,1)} %get-tuple-element.9, bf16[1,1024,1024]{2,1,0:T(8,128)(2,1)} %get-tuple-element.10, bf16[1,1024,1024]{2,1,0:T(8,128)(2,1)} %get-tuple-element.11, bf16[1,1024,1024]{2,1,0:T(8,128)(2,1)} %get-tuple-element.12, f32[256]{0:T(256)S(1)} %fusion.57, ...), kind=kOutput, calls=%fused_computation.52 | convolution fusion | flops 2701918208 | bytes 8914944 | tf_op jit(solution)/shard_map/qi,nik->nqk/dot_general | solution.py:92
  206.3 4.3 convert_bitcast_fusion.1
  210.6 6.2 %copy.80 = bf16[4,2048,256]{2,1,0:T(8,128)(2,1)} copy(bf16[4,2048,256]{1,2,0:T(8,128)(2,1)} %convert_bitcast_fusion.1) | data formatting | bytes 8388608 | tf_op jit(solution)/shard_map/convert_element_type | solution.py:99
  216.8 7.2 %reshape.116 = bf16[4,4,256,512]{3,2,1,0:T(8,128)(2,1)} reshape(bf16[4,2048,256]{2,1,0:T(8,128)(2,1)} %copy.80) | data formatting | bytes 8388608 | tf_op jit(solution)/shard_map/reshape | solution.py:100
  224.0 6.9 %convert_bitcast_fusion = bf16[4,4,256,512]{2,3,0,1:T(8,128)(2,1)} fusion(bf16[4,4,256,512]{3,2,1,0:T(8,128)(2,1)} %reshape.116, bf16[4,256,256]{1,2,0:T(8,128)(2,1)} %copy-done.6, bf16[4,256,256]{1,2,0:T(8,128)(2,1)S(1)} %copy-done.5, bf16[4,256,256]{1,2,0:T(8,128)(2,1)S(1)} %copy-done.3), kind=kOutput, calls=%fused_computation.12 | convolution fusion | flops 2157969408 | bytes 9961472 | tf_op jit(solution)/shard_map/noya,oab->noyb/dot_general | solution.py:101
  230.9 7.5 %copy.82 = bf16[4,4,256,512]{3,2,1,0:T(8,128)(2,1)} copy(bf16[4,4,256,512]{2,3,0,1:T(8,128)(2,1)} %convert_bitcast_fusion) | data formatting | bytes 8388608 | tf_op jit(solution)/shard_map/convert_element_type | solution.py:103
  238.4 5.4 copy.101
  251.4 2.7 fusion.21
  254.0 40.9 %copy.96 = bf16[2,4,256,256]{1,0,3,2:T(2,128)(2,1)} copy(bf16[2,4,256,256]{2,3,0,1:T(8,128)(2,1)S(1)} %fusion.21) | data formatting | bytes 2097152 | tf_op jit(solution)/shard_map/reshape | solution.py:121
  294.9 68.6 %reshape.133 = bf16[16,2,16384]{2,1,0:T(2,128)(2,1)} reshape(bf16[65536,2,4]{2,1,0:T(2,128)(2,1)} %bitcast.68) | data formatting | bytes 2097152
  363.5 5.1 all-to-all-start
  369.2 22.7 %all-to-all-done = bf16[16,2,16384]{2,1,0:T(2,128)(2,1)S(1)} async-done(((bf16[16,2,16384]{2,1,0:T(2,128)(2,1)}), bf16[16,2,16384]{2,1,0:T(2,128)(2,1)S(1)}, u32[]{:S(2)}, u32[]{:S(2)}) %all-to-all-start) | async-done | bytes 1048608 | tf_op jit(solution)/shard_map/all_to_all | solution.py:122
  391.8 73.1 %reshape.134 = bf16[65536,2,4]{2,1,0:T(2,128)(2,1)} reshape(bf16[16,2,16384]{2,1,0:T(2,128)(2,1)S(1)} %all-to-all-done) | data formatting | bytes 2097152
  464.9 46.7 %copy.97 = bf16[2,4,16,4096]{3,2,1,0:T(8,128)(2,1)S(1)} copy(bf16[2,4,16,4096]{1,0,3,2:T(2,128)(2,1)} %bitcast.69) | data formatting | bytes 2097152 | tf_op jit(solution)/shard_map/all_to_all | solution.py:122
  516.4 31.5 %all_to_all.27 = bf16[32,4,4096]{2,1,0:T(4,128)(2,1)S(1)} all-to-all(bf16[32,4,4096]{2,1,0:T(4,128)(2,1)S(1)} %copy.89), channel_id=1, replica_groups=mesh['groups'=2,'frames'=16] {'frames'}, dimensions={0} | all-to-all | bytes 2097152 | tf_op jit(solution)/shard_map/all_to_all | solution.py:127
  549.8 2.7 reshape.124
  552.5 2.9 copy.91
  (50 shorter events, 28.8 us)
Async XLA Ops:
  6.5 362.1 %copy-start = (bf16[32]{0:T(256)(128)(2,1)S(1)}, bf16[32]{0:T(256)(128)(2,1)}, u32[]{:S(2)}) copy-start(bf16[32]{0:T(256)(128)(2,1)} %param.7) | copy-start | bytes 196
  6.5 191.5 %all-reduce.3.cloned.1.call-start = ((), (), s32[]{:S(2)}) async-start(), calls=%async_computation.2 | async-start | bytes 16777216 | tf_op jit(solution)/shard_map/psum | solution.py:22
  30.2 2.5 copy-start.7
  45.7 6.4 %copy-start.1 = (bf16[2,4,256,512]{3,2,1,0:T(8,128)(2,1)S(1)}, bf16[2,4,256,512]{3,2,1,0:T(8,128)(2,1)}, u32[]{:S(2)}) copy-start(bf16[2,4,256,512]{3,2,1,0:T(8,128)(2,1)} %reshape.115) | copy-start | bytes 6291460
  51.0 0.8 copy-start.2
  51.0 1.0 copy-start.4
  51.0 1.1 copy-start.6
  216.8 7.2 %copy-start.3 = (bf16[4,256,256]{1,2,0:T(8,128)(2,1)S(1)}, bf16[4,256,256]{1,2,0:T(8,128)(2,1)}, u32[]{:S(2)}) copy-start(bf16[4,256,256]{1,2,0:T(8,128)(2,1)} %copy-done.2) | copy-start | bytes 1572868
  216.8 7.2 %copy-start.5 = (bf16[4,256,256]{1,2,0:T(8,128)(2,1)S(1)}, bf16[4,256,256]{1,2,0:T(8,128)(2,1)}, u32[]{:S(2)}) copy-start(bf16[4,256,256]{1,2,0:T(8,128)(2,1)} %copy-done.4) | copy-start | bytes 1572868
  363.5 28.3 %all-to-all-start = ((bf16[16,2,16384]{2,1,0:T(2,128)(2,1)}), bf16[16,2,16384]{2,1,0:T(2,128)(2,1)S(1)}, u32[]{:S(2)}, u32[]{:S(2)}) async-start(bf16[16,2,16384]{2,1,0:T(2,128)(2,1)} %reshape.133), calls=%async_computation | async-start | bytes 2097152 | tf_op jit(solution)/shard_map/all_to_all | solution.py:122
Sparse Core Ops, SparseCore 0:
  25.7 172.2 all-reduce.2
where the time goes:
time: 575 us; the launch traced here: 566 us
  local copies, waits for them, and re-layouts  283 us (49%)
  waiting for transfers between devices  167 us (29%)
  matrix products  31.9 us (6%)
  blocking collectives  31.5 us (5%)
  between operations  24 us (4%)
  other arithmetic  23.7 us (4%)
    unnamed x22, local copies, waits for them, and re-layouts  152 us
    psum x1, waiting for transfers between devices, spread(): return lax.psum(jnp.where(mine, x, jnp.zeros_like(x)), axis)  144 us
    all_to_all x3, local copies, waits for them, and re-layouts, body(): lax.all_to_all(phase_signal, 'frames', split_axis=2, concat_axis=0, tiled...  50.2 us
    reshape x1, local copies, waits for them, and re-layouts, body(): phase_signal = phase_signal.reshape(frames_here, ORIENT, QUART * QUART)  40.9 us
    all_to_all x1, blocking collectives, body(): lax.all_to_all(filtered, 'frames', split_axis=0, concat_axis=2, tiled=True)  31.5 us
    all_to_all x1, waiting for transfers between devices, body(): lax.all_to_all(phase_signal, 'frames', split_axis=2, concat_axis=0, tiled...  22.7 us
  transfers between devices with their start and end apart: 2, of which 2 were waited for; matrix products, arithmetic and copies ran while one was open for 5% of the time, Pallas kernels for 0%

commit v1 on v0

--- a/solution.py
+++ b/solution.py
@@ -1,8 +1,11 @@
 import math
 
 import jax
+import numpy as np
 import jax.numpy as jnp
 from jax import lax
+from jax.experimental import pallas as pl
+from jax.experimental.pallas import tpu as pltpu
 from jax.sharding import PartitionSpec as P
 
 IMG = 1024
@@ -129,7 +132,298 @@
     return jnp.sum(amplitude * filtered, axis=1) / (jnp.sum(amplitude, axis=1) + 1.0)
 
 
+REACH = 32
+
+
+def down_table():
+    position = np.arange(QUART, dtype=np.float32)[:, None]
+    columns = np.arange(IMG, dtype=np.float32)[None, :]
+    offset = columns - np.float32(4.0) * position - np.float32(1.5)
+    weight = np.exp(-offset * offset / np.float32(2.0 * blur_sigma * blur_sigma))
+    return (weight / np.sum(weight, axis=1, keepdims=True)).astype(jnp.bfloat16)
+
+
+def waves():
+    angles = np.arange(ORIENT, dtype=np.float32) * np.float32(math.pi / ORIENT)
+    return np.float32(wave_number) * np.cos(angles), np.float32(wave_number) * np.sin(angles)
+
+
+def gabor_envelope(offset):
+    return np.float32(gabor_gain) * np.exp(-offset * offset / np.float32(2.0 * gabor_sigma * gabor_sigma))
+
+
+def left_window(rows):
+    offset = (
+        np.arange(rows + 2 * REACH, dtype=np.float32)[None, :]
+        - REACH
+        - np.arange(rows, dtype=np.float32)[:, None]
+    )
+    envelope = gabor_envelope(offset)
+    phase = waves()[1][:, None, None] * offset[None]
+    table = np.stack([envelope * np.cos(phase), envelope * np.sin(phase)], axis=1)
+    return table.reshape(ORIENT * 2 * rows, -1).astype(jnp.bfloat16)
+
+
+def right_tables():
+    position = np.arange(QUART, dtype=np.float32)
+    offset = position[:, None] - position[None, :]
+    envelope = gabor_envelope(offset)
+    phase = waves()[0][:, None, None] * offset[None]
+    real, imag = envelope * np.cos(phase), envelope * np.sin(phase)
+    upper = np.concatenate([real, imag], axis=2)
+    lower = np.concatenate([-imag, real], axis=2)
+    return np.stack([upper, lower], axis=1).astype(jnp.bfloat16)
+
+
+def make_kernel(parts, here, rows):
+    frames = parts * here
+    window = rows + 2 * REACH
+    total = frames * rows
+
+    def kernel(
+        refs, taps, video_hbm, down_hbm, down_t_hbm, left, right_hbm, out,
+        video, down, down_t, right, half, reduced, gathered, stacked, coeffs,
+        phase, matrix, numer, denom, moved, landed,
+        load_sem, send_a, recv_a, send_b, recv_b,
+    ):
+        me = lax.axis_index("frames")
+        barrier = pltpu.get_barrier_semaphore()
+
+        def peer(j):
+            return lax.rem(me + j, parts)
+
+        def source(j):
+            return lax.rem(me + parts - j, parts)
+
+        loads = [
+            pltpu.make_async_copy(down_t_hbm, down_t, load_sem.at[0]),
+        ]
+        for n in range(here):
+            loads.append(pltpu.make_async_copy(video_hbm.at[n], video.at[n], load_sem.at[1 + n]))
+        loads.append(pltpu.make_async_copy(down_hbm, down, load_sem.at[1 + here]))
+        loads.append(pltpu.make_async_copy(right_hbm, right, load_sem.at[2 + here]))
+        for copy in loads:
+            copy.start()
+
+        @pl.loop(1, parts)
+        def _(j):
+            pl.semaphore_signal(barrier, inc=1, device_id={"frames": peer(j)})
+
+        edge = jnp.zeros((here, REACH, QUART), jnp.bfloat16)
+        reduced[:, :REACH, :] = edge
+        reduced[:, REACH + QUART :, :] = edge
+
+        loads[0].wait()
+        for n in range(here):
+            loads[1 + n].wait()
+            half[n] = jnp.dot(
+                video[n], down_t[...], preferred_element_type=jnp.float32
+            ).astype(jnp.bfloat16)
+        loads[1 + here].wait()
+        for n in range(here):
+            reduced[n, REACH : REACH + QUART, :] = jnp.dot(
+                down[...], half[n], preferred_element_type=jnp.float32
+            ).astype(jnp.bfloat16)
+
+        pl.semaphore_wait(barrier, parts - 1)
+
+        def spread_copy(j):
+            to = peer(j)
+            return pltpu.make_async_remote_copy(
+                src_ref=reduced.at[:, pl.ds(pl.multiple_of(to * rows, rows), window), :],
+                dst_ref=gathered.at[pl.ds(me * here, here)],
+                send_sem=send_a.at[j],
+                recv_sem=recv_a.at[j],
+                device_id={"frames": to},
+            )
+
+        @pl.loop(1, parts)
+        def _(j):
+            spread_copy(j).start()
+
+        lag = lax.broadcasted_iota(jnp.int32, (frames, frames), 0) - lax.broadcasted_iota(
+            jnp.int32, (frames, frames), 1
+        )
+        toeplitz = jnp.zeros((frames, frames), jnp.float32)
+        tap_row = taps[...].astype(jnp.float32)
+        for k in range(min(taps.shape[1], frames)):
+            toeplitz = jnp.where(lag == k, tap_row[:, k : k + 1], toeplitz)
+        owner = lax.broadcasted_iota(jnp.int32, (total, frames), 0) // rows
+        repeat = jnp.where(
+            owner == lax.broadcasted_iota(jnp.int32, (total, frames), 1), 1.0, 0.0
+        ).astype(jnp.bfloat16)
+        tall = jnp.dot(
+            repeat, toeplitz.astype(jnp.bfloat16), preferred_element_type=jnp.float32
+        ).astype(jnp.bfloat16)
+        wide = lax.dot_general(
+            tall, repeat, (((1,), (1,)), ((), ())), preferred_element_type=jnp.float32
+        )
+        same = (
+            lax.broadcasted_iota(jnp.int32, (total, total), 0) % rows
+            == lax.broadcasted_iota(jnp.int32, (total, total), 1) % rows
+        )
+        matrix[...] = jnp.where(same, wide, 0.0).astype(jnp.bfloat16)
+
+        def stack_one(t, block):
+            stacked[t] = (
+                jnp.dot(left[...], block, preferred_element_type=jnp.float32)
+                .astype(jnp.bfloat16)
+                .reshape(ORIENT * 2, rows, QUART)
+            )
+
+        own = pl.ds(pl.multiple_of(me * rows, rows), window)
+        for n in range(here):
+            stack_one(me * here + n, reduced[n, own, :])
+
+        @pl.loop(1, parts)
+        def _(j):
+            spread_copy(j).wait_recv()
+            base = source(j) * here
+            for n in range(here):
+                stack_one(base + n, gathered[base + n])
+
+        loads[2 + here].wait()
+        step = frames // 4
+        for o in range(ORIENT):
+            for part in range(4):
+                where = slice(part * step, (part + 1) * step)
+                value = jnp.dot(
+                    stacked[where, 2 * o].reshape(step * rows, QUART),
+                    right[o, 0],
+                    preferred_element_type=jnp.float32,
+                ) + jnp.dot(
+                    stacked[where, 2 * o + 1].reshape(step * rows, QUART),
+                    right[o, 1],
+                    preferred_element_type=jnp.float32,
+                )
+                coeffs[where, o] = value.astype(jnp.bfloat16).reshape(step, rows, 2 * QUART)
+
+        @pl.loop(0, frames)
+        def _(t):
+            ref = refs[t]
+            ones = coeffs[t].astype(jnp.float32)
+            base = coeffs[ref].astype(jnp.float32)
+            real, imag = ones[..., :QUART], ones[..., QUART:]
+            ref_real, ref_imag = base[..., :QUART], base[..., QUART:]
+            prod_real = real * ref_real + imag * ref_imag
+            prod_imag = imag * ref_real - real * ref_imag
+            signal = prod_imag * lax.rsqrt(prod_real * prod_real + prod_imag * prod_imag + 1.0)
+            phase[:, t] = signal.astype(jnp.bfloat16)
+            denom[t] = jnp.sum(real * real + imag * imag, axis=0) + 1.0
+
+        for o in range(ORIENT):
+            filtered = (
+                jnp.dot(
+                    matrix[...],
+                    phase[o].reshape(total, QUART),
+                    preferred_element_type=jnp.float32,
+                )
+                .astype(jnp.bfloat16)
+                .astype(jnp.float32)
+                .reshape(frames, rows, QUART)
+            )
+            real = coeffs[:, o, :, :QUART].astype(jnp.float32)
+            imag = coeffs[:, o, :, QUART:].astype(jnp.float32)
+            term = (real * real + imag * imag) * filtered
+            if o == 0:
+                numer[...] = term
+            elif o < ORIENT - 1:
+                numer[...] += term
+            else:
+                moved[...] = ((numer[...] + term) / denom[...]).astype(jnp.bfloat16)
+
+        here_rows = pl.ds(pl.multiple_of(me * rows, rows), rows)
+
+        def return_copy(j):
+            to = peer(j)
+            return pltpu.make_async_remote_copy(
+                src_ref=moved.at[pl.ds(to * here, here)],
+                dst_ref=landed.at[:, here_rows, :],
+                send_sem=send_b.at[j],
+                recv_sem=recv_b.at[j],
+                device_id={"frames": to},
+            )
+
+        @pl.loop(1, parts)
+        def _(j):
+            return_copy(j).start()
+
+        landed[:, here_rows, :] = moved[pl.ds(me * here, here)]
+
+        @pl.loop(1, parts)
+        def _(j):
+            spread_copy(j).wait_send()
+
+        @pl.loop(1, parts)
+        def _(j):
+            return_copy(j).wait_recv()
+
+        out[...] = landed[...].astype(jnp.float32)
+
+        @pl.loop(1, parts)
+        def _(j):
+            return_copy(j).wait_send()
+
+    bf16, f32, dma = jnp.bfloat16, jnp.float32, pltpu.SemaphoreType.DMA
+    anywhere = pl.BlockSpec(memory_space=pl.ANY)
+    vmem = pl.BlockSpec(memory_space=pltpu.VMEM)
+    return pl.pallas_call(
+        kernel,
+        out_shape=jax.ShapeDtypeStruct((here, QUART, QUART), f32),
+        in_specs=[pl.BlockSpec(memory_space=pltpu.SMEM), vmem, anywhere, anywhere, anywhere, vmem, anywhere],
+        out_specs=vmem,
+        scratch_shapes=[
+            pltpu.VMEM((here, IMG, IMG), bf16),
+            pltpu.VMEM((QUART, IMG), bf16),
+            pltpu.VMEM((IMG, QUART), bf16),
+            pltpu.VMEM((ORIENT, 2, QUART, 2 * QUART), bf16),
+            pltpu.VMEM((here, IMG, QUART), bf16),
+            pltpu.VMEM((here, QUART + 2 * REACH, QUART), bf16),
+            pltpu.VMEM((frames, window, QUART), bf16),
+            pltpu.VMEM((frames, ORIENT * 2, rows, QUART), bf16),
+            pltpu.VMEM((frames, ORIENT, rows, 2 * QUART), bf16),
+            pltpu.VMEM((ORIENT, frames, rows, QUART), bf16),
+            pltpu.VMEM((total, total), bf16),
+            pltpu.VMEM((frames, rows, QUART), f32),
+            pltpu.VMEM((frames, rows, QUART), f32),
+            pltpu.VMEM((frames, rows, QUART), bf16),
+            pltpu.VMEM((here, QUART, QUART), bf16),
+            dma((3 + here,)),
+            dma((parts,)),
+            dma((parts,)),
+            dma((parts,)),
+            dma((parts,)),
+        ],
+        compiler_params=pltpu.CompilerParams(
+            collective_id=0, has_side_effects=True, vmem_limit_bytes=60 * 1024 * 1024
+        ),
+    )
+
+
+def kernel_body(parts, video_frames, segments, ref_pick, band_taps):
+    here = video_frames.shape[0]
+    rows = QUART // parts
+    ref_frames = segment_refs(segments, ref_pick, NSEG)
+    numbers = jnp.arange(NSEG, dtype=jnp.int32)
+    per_frame = jnp.sum(jnp.where(segments[:, None] == numbers[None, :], ref_frames[None, :], 0), axis=1)
+    down = down_table()
+    return make_kernel(parts, here, rows)(
+        per_frame.astype(jnp.int32),
+        band_taps[None, :],
+        video_frames,
+        jnp.asarray(down),
+        jnp.asarray(np.ascontiguousarray(down.T)),
+        jnp.asarray(left_window(rows)),
+        jnp.asarray(right_tables()),
+    )
+
+
 def solution(mesh):
+    parts = mesh.shape["frames"]
+    if QUART % parts == 0 and (QUART // parts) % 16 == 0:
+        chosen = lambda *args: kernel_body(parts, *args)
+    else:
+        chosen = body
     in_specs = (P(("groups", "frames"), None, None), P("groups"), P("groups"), P())
     out_specs = P(("groups", "frames"), None, None)
-    return jax.shard_map(body, mesh=mesh, in_specs=in_specs, out_specs=out_specs, check_vma=False)
+    return jax.shard_map(chosen, mesh=mesh, in_specs=in_specs, out_specs=out_specs, check_vma=False)

time: 575 us -> 53.4 us (0.09); the launches traced: 566 us -> 52.8 us
  local copies, waits for them, and re-layouts: 283 us -> 1.87 us
  waiting for transfers between devices: 167 us -> 0 us
  Pallas kernels: 0 us -> 48.1 us
  matrix products: 31.9 us -> 0 us
  blocking collectives: 31.5 us -> 0 us
  between operations: 24 us -> 0.01 us
  other arithmetic: 23.7 us -> 2.84 us
    unnamed x22 -> x1, local copies, waits for them, and re-layouts: 152 us -> 1.87 us
    psum x1 -> x0, waiting for transfers between devices: 144 us -> none  [spread(): return lax.psum(jnp.where(mine, x, jnp.zeros_like(x)), axis)]
    reshape x3 -> x0, local copies, waits for them, and re-layouts: 50.3 us -> none  [the longest x1 40.9 us: body(): phase_signal = phase_signal.reshape(frames_here, ORIENT, QUART * QUART)]
    all_to_all x3 -> x0, local copies, waits for them, and re-layouts: 50.2 us -> none  [body(): lax.all_to_all(phase_signal, 'frames', split_axis=2, concat_axis=0, tiled...]
    pallas_call x0 -> x1, Pallas kernels: none -> 48.1 us  [kernel_body(): make_kernel(parts, here, rows)]
    dot_general x9 -> x0, matrix products: 31.9 us -> none  [the longest x2 8.56 us: filter_frames(): jnp.einsum('noya,oab->noyb', stacked, right_table, preferred_element_type...]
    all_to_all x1 -> x0, blocking collectives: 31.5 us -> none  [body(): lax.all_to_all(filtered, 'frames', split_axis=0, concat_axis=2, tiled=True)]
    convert_element_type x8 -> x0, local copies, waits for them, and re-layouts: 25.4 us -> none  [the longest x2 9.14 us: filter_frames(): stacked = jnp.einsum('ra,nak->nrk', left_table, reduced, preferred_elemen...]
  transfers between devices with their start and end apart: 2 -> 0, of which waited for: 2 -> 0; matrix products, arithmetic and copies ran while one was open for 5% -> 0% of each run, Pallas kernels for 0% -> 0%
where the time goes in v1:
time: 53.4 us; the launch traced here: 52.8 us
  Pallas kernels  48.1 us (90%)
  other arithmetic  2.84 us (5%)
  local copies, waits for them, and re-layouts  1.87 us (4%)
    pallas_call x1, Pallas kernels, kernel_body(): make_kernel(parts, here, rows)  48.1 us
    unnamed x1, local copies, waits for them, and re-layouts  1.87 us
    reduce_sum x1, other arithmetic, kernel_body(): jnp.sum(jnp.where(segments[:, None] == numbers[None, :], ref_frames[None,...  1.25 us

profile of v1, /device:TPU:1, one launch (start us, length us, event | category | flops | bytes accessed | tf_op | source)
XLA Modules:
  0.0 52.8 jit_solution(13357284717283966190)
XLA Ops:
  0.0 0.8 %convert_reduce_fusion = (s32[4]{0:T(128)S(1)}, s32[4]{0:T(128)S(1)}) fusion(s32[32]{0:T(128)} %param.9), kind=kLoop, calls=%fused_computation.2 | loop fusion | flops 760 | bytes 160 | tf_op jit(solution)/shard_map/reduce_sum | solution.py:82
  0.8 0.8 %fusion = s32[4]{0:T(128)S(1)} fusion(s32[4]{0:T(128)S(1)} %get-tuple-element.6, s32[4]{0:T(128)} %param.10, s32[4]{0:T(128)S(1)} %get-tuple-element.5), kind=kLoop, calls=%fused_computation.8 | loop fusion | flops 44 | bytes 64 | tf_op jit(solution)/shard_map/add | solution.py:83
  1.6 1.2 %select_reduce_fusion.refs = s32[32]{0:T(128)} fusion(s32[4]{0:T(128)S(1)} %fusion, s32[32]{0:T(128)} %param.9), kind=kLoop, calls=%fused_computation.1 | loop fusion | flops 352 | bytes 272 | tf_op jit(solution)/shard_map/reduce_sum | solution.py:408
  2.8 48.1 %shard_map.82 = f32[2,256,256]{2,1,0:T(8,128)} custom-call(s32[32]{0:T(128)} %select_reduce_fusion.refs, bf16[1,32]{1,0:T(2,128)(2,1)} %bitcast.1, bf16[2,1024,1024]{2,1,0:T(8,128)(2,1)} %video_hbm.1, bf16[256,1024]{1,0:T(8,128)(2,1)} %constant.15.clone.down_hbm, bf16[1024,256]{1,0:T(8,128)(2,1)} %constant.16.clone.down_t_hbm, ...), custom_call_target="tpu_custom_call" | custom-call | tf_op jit(solution)/shard_map/pallas_call | solution.py:410
  50.9 1.9 %copy.10 = f32[2,256,256]{2,1,0:T(8,128)} copy(f32[2,256,256]{2,1,0:T(8,128)} %shard_map.82) | data formatting | bytes 1048576

commit v2 on v1

--- a/solution.py
+++ b/solution.py
@@ -132,6 +132,7 @@
     return jnp.sum(amplitude * filtered, axis=1) / (jnp.sum(amplitude, axis=1) + 1.0)
 
 
+PICK_LIMIT = 4096
 REACH = 32
 
 
@@ -175,35 +176,59 @@
     return np.stack([upper, lower], axis=1).astype(jnp.bfloat16)
 
 
+PLANE = 4
+PAIR = 2
+
+
+def flip(number, bits):
+    step = 1
+    while step <= bits:
+        if bits & step:
+            number = number + step - 2 * step * ((number // step) % 2)
+        step *= 2
+    return number
+
+
 def make_kernel(parts, here, rows):
     frames = parts * here
+    planes = parts // PLANE
     window = rows + 2 * REACH
+    pair_window = PAIR * rows + 2 * REACH
+    plane_window = PLANE * rows + 2 * REACH
     total = frames * rows
+    chunks = 2
 
     def kernel(
-        refs, taps, video_hbm, down_hbm, down_t_hbm, left, right_hbm, out,
+        segments, picks, taps, video_hbm, down_hbm, down_t_hbm, left, right_hbm, out_hbm,
         video, down, down_t, right, half, reduced, gathered, stacked, coeffs,
-        phase, matrix, numer, denom, moved, landed,
-        load_sem, send_a, recv_a, send_b, recv_b,
+        phase, matrix, numer, denom, moved, landed, out,
+        load_sem, store_sem, send_1, recv_1, send_2, recv_2, send_3, recv_3, send_b, recv_b,
     ):
         me = lax.axis_index("frames")
+        plane, spot = me // PLANE, me % PLANE
+        across, sibling = flip(spot, PAIR), flip(spot, 1)
         barrier = pltpu.get_barrier_semaphore()
 
         def peer(j):
             return lax.rem(me + j, parts)
 
-        def source(j):
-            return lax.rem(me + parts - j, parts)
-
-        loads = [
-            pltpu.make_async_copy(down_t_hbm, down_t, load_sem.at[0]),
-        ]
+        def piece(n, part):
+            height = IMG // chunks
+            where = pl.ds(part * height, height)
+            return pltpu.make_async_copy(
+                video_hbm.at[n, where], video.at[n, where], load_sem.at[3 + n * chunks + part]
+            )
+
+        load_down_t = pltpu.make_async_copy(down_t_hbm, down_t, load_sem.at[0])
+        load_down = pltpu.make_async_copy(down_hbm, down, load_sem.at[1])
+        load_right = pltpu.make_async_copy(right_hbm, right, load_sem.at[2])
+        load_down_t.start()
         for n in range(here):
-            loads.append(pltpu.make_async_copy(video_hbm.at[n], video.at[n], load_sem.at[1 + n]))
-        loads.append(pltpu.make_async_copy(down_hbm, down, load_sem.at[1 + here]))
-        loads.append(pltpu.make_async_copy(right_hbm, right, load_sem.at[2 + here]))
-        for copy in loads:
-            copy.start()
+            for part in range(chunks):
+                piece(n, part).start()
+            if n == 0:
+                load_down.start()
+        load_right.start()
 
         @pl.loop(1, parts)
         def _(j):
@@ -213,33 +238,77 @@
         reduced[:, :REACH, :] = edge
         reduced[:, REACH + QUART :, :] = edge
 
-        loads[0].wait()
+        def frame_of(j, where, n):
+            return (flip(plane, j) * PLANE + where) * here + n
+
+        def rows_of(j, n, first, size):
+            if j == 0:
+                start = pl.multiple_of((plane * PLANE + first) * rows, rows)
+                return reduced.at[n, pl.ds(start, size), :]
+            return gathered.at[frame_of(j, spot, n), pl.ds(pl.multiple_of(first * rows, rows), size), :]
+
+        def copy_1(j, n):
+            to = flip(plane, j)
+            start = pl.multiple_of(to * PLANE * rows, rows)
+            return pltpu.make_async_remote_copy(
+                src_ref=reduced.at[n, pl.ds(start, plane_window), :],
+                dst_ref=gathered.at[me * here + n],
+                send_sem=send_1.at[j, n],
+                recv_sem=recv_1.at[j, n],
+                device_id={"frames": to * PLANE + spot},
+            )
+
+        def copy_2(j, n):
+            first = across // PAIR * PAIR
+            where = pl.ds(pl.multiple_of(first * rows, rows), pair_window)
+            return pltpu.make_async_remote_copy(
+                src_ref=rows_of(j, n, first, pair_window),
+                dst_ref=gathered.at[frame_of(j, spot, n), where, :],
+                send_sem=send_2.at[j, n],
+                recv_sem=recv_2.at[j, n],
+                device_id={"frames": plane * PLANE + across},
+            )
+
+        sibling_rows = pl.ds(pl.multiple_of(sibling * rows, rows), window)
+
+        def copy_3(j, n):
+            return pltpu.make_async_remote_copy(
+                src_ref=rows_of(j, n, sibling, window),
+                dst_ref=gathered.at[frame_of(j, spot, n), sibling_rows, :],
+                send_sem=send_3.at[j, n],
+                recv_sem=recv_3.at[j, n],
+                device_id={"frames": plane * PLANE + sibling},
+            )
+
+        def copy_4(j, n):
+            part = gathered.at[frame_of(j, across, n), sibling_rows, :]
+            return pltpu.make_async_remote_copy(
+                src_ref=part,
+                dst_ref=part,
+                send_sem=send_3.at[planes + j, n],
+                recv_sem=recv_3.at[planes + j, n],
+                device_id={"frames": plane * PLANE + sibling},
+            )
+
+        load_down_t.wait()
         for n in range(here):
-            loads[1 + n].wait()
-            half[n] = jnp.dot(
-                video[n], down_t[...], preferred_element_type=jnp.float32
-            ).astype(jnp.bfloat16)
-        loads[1 + here].wait()
-        for n in range(here):
+            for part in range(chunks):
+                piece(n, part).wait()
+                where = slice(part * (IMG // chunks), (part + 1) * (IMG // chunks))
+                half[n, where] = jnp.dot(
+                    video[n, where], down_t[...], preferred_element_type=jnp.float32
+                ).astype(jnp.bfloat16)
+            if n == 0:
+                load_down.wait()
             reduced[n, REACH : REACH + QUART, :] = jnp.dot(
                 down[...], half[n], preferred_element_type=jnp.float32
             ).astype(jnp.bfloat16)
-
-        pl.semaphore_wait(barrier, parts - 1)
-
-        def spread_copy(j):
-            to = peer(j)
-            return pltpu.make_async_remote_copy(
-                src_ref=reduced.at[:, pl.ds(pl.multiple_of(to * rows, rows), window), :],
-                dst_ref=gathered.at[pl.ds(me * here, here)],
-                send_sem=send_a.at[j],
-                recv_sem=recv_a.at[j],
-                device_id={"frames": to},
-            )
-
-        @pl.loop(1, parts)
-        def _(j):
-            spread_copy(j).start()
+            if n == 0:
+                pl.semaphore_wait(barrier, parts - 1)
+            for j in range(1, planes):
+                copy_1(j, n).start()
+            copy_2(0, n).start()
+            copy_3(0, n).start()
 
         lag = lax.broadcasted_iota(jnp.int32, (frames, frames), 0) - lax.broadcasted_iota(
             jnp.int32, (frames, frames), 1
@@ -271,18 +340,40 @@
                 .reshape(ORIENT * 2, rows, QUART)
             )
 
-        own = pl.ds(pl.multiple_of(me * rows, rows), window)
+        own_rows = pl.ds(pl.multiple_of(spot * rows, rows), window)
+
+        def stack_arrived(j, where):
+            @pl.loop(0, here)
+            def _(n):
+                t = frame_of(j, where, n)
+                stack_one(t, gathered[t, own_rows, :])
+
+        def second(j):
+            for n in range(here):
+                copy_2(j, n).wait_recv()
+                copy_4(j, n).start()
+            stack_arrived(j, across)
+
         for n in range(here):
-            stack_one(me * here + n, reduced[n, own, :])
-
-        @pl.loop(1, parts)
-        def _(j):
-            spread_copy(j).wait_recv()
-            base = source(j) * here
+            stack_one(me * here + n, reduced[n, pl.ds(pl.multiple_of(me * rows, rows), window), :])
+        for j in range(1, planes):
             for n in range(here):
-                stack_one(base + n, gathered[base + n])
-
-        loads[2 + here].wait()
+                copy_1(j, n).wait_recv()
+                copy_2(j, n).start()
+                copy_3(j, n).start()
+            stack_arrived(j, spot)
+            second(j - 1)
+        for j in range(planes):
+            for n in range(here):
+                copy_3(j, n).wait_recv()
+            stack_arrived(j, sibling)
+        second(planes - 1)
+        for j in range(planes):
+            for n in range(here):
+                copy_4(j, n).wait_recv()
+            stack_arrived(j, flip(across, 1))
+
+        load_right.wait()
         step = frames // 4
         for o in range(ORIENT):
             for part in range(4):
@@ -298,9 +389,23 @@
                 )
                 coeffs[where, o] = value.astype(jnp.bfloat16).reshape(step, rows, 2 * QUART)
 
+        counts = [jnp.int32(0)] * NSEG
+        for t in range(frames):
+            for s in range(NSEG):
+                counts[s] = counts[s] + jnp.where(segments[t] == s, 1, 0)
+        picked, first = [], jnp.int32(0)
+        for s in range(NSEG):
+            rest = picks[s]
+            for bit in reversed(range((PICK_LIMIT - 1).bit_length())):
+                rest = jnp.where(rest >= counts[s] * (1 << bit), rest - counts[s] * (1 << bit), rest)
+            picked.append(first + rest)
+            first = first + counts[s]
+
         @pl.loop(0, frames)
         def _(t):
-            ref = refs[t]
+            ref = picked[NSEG - 1]
+            for s in range(NSEG - 1):
+                ref = jnp.where(segments[t] == s, picked[s], ref)
             ones = coeffs[t].astype(jnp.float32)
             base = coeffs[ref].astype(jnp.float32)
             real, imag = ones[..., :QUART], ones[..., QUART:]
@@ -350,28 +455,37 @@
 
         landed[:, here_rows, :] = moved[pl.ds(me * here, here)]
 
-        @pl.loop(1, parts)
-        def _(j):
-            spread_copy(j).wait_send()
+        for n in range(here):
+            for j in range(planes):
+                if j:
+                    copy_1(j, n).wait_send()
+                copy_2(j, n).wait_send()
+                copy_3(j, n).wait_send()
+                copy_4(j, n).wait_send()
 
         @pl.loop(1, parts)
         def _(j):
             return_copy(j).wait_recv()
 
         out[...] = landed[...].astype(jnp.float32)
+        store = pltpu.make_async_copy(out, out_hbm, store_sem)
+        store.start()
 
         @pl.loop(1, parts)
         def _(j):
             return_copy(j).wait_send()
 
+        store.wait()
+
     bf16, f32, dma = jnp.bfloat16, jnp.float32, pltpu.SemaphoreType.DMA
     anywhere = pl.BlockSpec(memory_space=pl.ANY)
     vmem = pl.BlockSpec(memory_space=pltpu.VMEM)
+    smem = pl.BlockSpec(memory_space=pltpu.SMEM)
     return pl.pallas_call(
         kernel,
         out_shape=jax.ShapeDtypeStruct((here, QUART, QUART), f32),
-        in_specs=[pl.BlockSpec(memory_space=pltpu.SMEM), vmem, anywhere, anywhere, anywhere, vmem, anywhere],
-        out_specs=vmem,
+        in_specs=[smem, smem, vmem, anywhere, anywhere, anywhere, vmem, anywhere],
+        out_specs=anywhere,
         scratch_shapes=[
             pltpu.VMEM((here, IMG, IMG), bf16),
             pltpu.VMEM((QUART, IMG), bf16),
@@ -379,7 +493,7 @@
             pltpu.VMEM((ORIENT, 2, QUART, 2 * QUART), bf16),
             pltpu.VMEM((here, IMG, QUART), bf16),
             pltpu.VMEM((here, QUART + 2 * REACH, QUART), bf16),
-            pltpu.VMEM((frames, window, QUART), bf16),
+            pltpu.VMEM((frames, plane_window, QUART), bf16),
             pltpu.VMEM((frames, ORIENT * 2, rows, QUART), bf16),
             pltpu.VMEM((frames, ORIENT, rows, 2 * QUART), bf16),
             pltpu.VMEM((ORIENT, frames, rows, QUART), bf16),
@@ -388,9 +502,15 @@
             pltpu.VMEM((frames, rows, QUART), f32),
             pltpu.VMEM((frames, rows, QUART), bf16),
             pltpu.VMEM((here, QUART, QUART), bf16),
-            dma((3 + here,)),
-            dma((parts,)),
-            dma((parts,)),
+            pltpu.VMEM((here, QUART, QUART), f32),
+            dma((3 + here * chunks,)),
+            dma,
+            dma((planes, here)),
+            dma((planes, here)),
+            dma((planes, here)),
+            dma((planes, here)),
+            dma((2 * planes, here)),
+            dma((2 * planes, here)),
             dma((parts,)),
             dma((parts,)),
         ],
@@ -403,12 +523,10 @@
 def kernel_body(parts, video_frames, segments, ref_pick, band_taps):
     here = video_frames.shape[0]
     rows = QUART // parts
-    ref_frames = segment_refs(segments, ref_pick, NSEG)
-    numbers = jnp.arange(NSEG, dtype=jnp.int32)
-    per_frame = jnp.sum(jnp.where(segments[:, None] == numbers[None, :], ref_frames[None, :], 0), axis=1)
     down = down_table()
     return make_kernel(parts, here, rows)(
-        per_frame.astype(jnp.int32),
+        segments,
+        ref_pick,
         band_taps[None, :],
         video_frames,
         jnp.asarray(down),
@@ -420,7 +538,7 @@
 
 def solution(mesh):
     parts = mesh.shape["frames"]
-    if QUART % parts == 0 and (QUART // parts) % 16 == 0:
+    if QUART % parts == 0 and (QUART // parts) % 16 == 0 and parts in (4, 8, 16):
         chosen = lambda *args: kernel_body(parts, *args)
     else:
         chosen = body

time: 53.4 us -> 38.4 us (0.72)
  Pallas kernels: 48.1 us -> 36.3 us
  other arithmetic: 2.84 us -> 0 us
    pallas_call x1, Pallas kernels: 48.1 us -> 36.3 us  [kernel_body(): make_kernel(parts, here, rows)]
    reduce_sum x2 -> x0, other arithmetic: 2.05 us -> none  [the longest x1 1.25 us: kernel_body(): jnp.sum(jnp.where(segments[:, None] == numbers[None, :], ref_frames[None,...]
    add x1 -> x0, other arithmetic: 0.79 us -> none  [segment_refs(): return starts + ref_pick % counts]
where the time goes in v2:
time: 38.4 us; the launch traced here: 38.2 us
  Pallas kernels  36.3 us (95%)
  local copies, waits for them, and re-layouts  1.87 us (5%)
    pallas_call x1, Pallas kernels, kernel_body(): make_kernel(parts, here, rows)  36.3 us
    unnamed x1, local copies, waits for them, and re-layouts  1.87 us

profile of v2, /device:TPU:1, one launch (start us, length us, event | category | flops | bytes accessed | tf_op | source)
XLA Modules:
  0.0 38.2 jit_solution(7466072130347498880)
XLA Ops:
  0.0 36.3 %shard_map.82 = f32[2,256,256]{2,1,0:T(8,128)} custom-call(s32[32]{0:T(128)} %segments.1, s32[4]{0:T(128)} %picks.1, bf16[1,32]{1,0:T(2,128)(2,1)} %bitcast.1, bf16[2,1024,1024]{2,1,0:T(8,128)(2,1)} %video_hbm.1, bf16[256,1024]{1,0:T(8,128)(2,1)} %constant.8.clone.down_hbm, bf16[1024,256]{1,0:T(8,128)(2,1)} %constant.9.clone.down_t_hbm, ...), custom_call_target="tpu_custom_call" | custom-call | tf_op jit(solution)/shard_map/pallas_call | solution.py:527
  36.3 1.9 %copy.10 = f32[2,256,256]{2,1,0:T(8,128)} copy(f32[2,256,256]{2,1,0:T(8,128)} %shard_map.82) | data formatting | bytes 1048576

commit v3 on v2

--- a/solution.py
+++ b/solution.py
@@ -201,7 +201,7 @@
     def kernel(
         segments, picks, taps, video_hbm, down_hbm, down_t_hbm, left, right_hbm, out_hbm,
         video, down, down_t, right, half, reduced, gathered, stacked, coeffs,
-        phase, matrix, numer, denom, moved, landed, out,
+        phase, matrix, numer, denom, moved,
         load_sem, store_sem, send_1, recv_1, send_2, recv_2, send_3, recv_3, send_b, recv_b,
     ):
         me = lax.axis_index("frames")
@@ -230,6 +230,16 @@
                 load_down.start()
         load_right.start()
 
+        blank = jnp.zeros((frames, REACH, QUART), jnp.bfloat16)
+
+        @pl.when(plane == 0)
+        def _():
+            gathered[:, :REACH, :] = blank
+
+        @pl.when(plane == planes - 1)
+        def _():
+            gathered[:, plane_window - REACH :, :] = blank
+
         @pl.loop(1, parts)
         def _(j):
             pl.semaphore_signal(barrier, inc=1, device_id={"frames": peer(j)})
@@ -247,16 +257,31 @@
                 return reduced.at[n, pl.ds(start, size), :]
             return gathered.at[frame_of(j, spot, n), pl.ds(pl.multiple_of(first * rows, rows), size), :]
 
-        def copy_1(j, n):
+        def copy_1(j, n, low, high):
             to = flip(plane, j)
-            start = pl.multiple_of(to * PLANE * rows, rows)
+            start = pl.multiple_of(to * PLANE * rows + low, rows)
             return pltpu.make_async_remote_copy(
-                src_ref=reduced.at[n, pl.ds(start, plane_window), :],
-                dst_ref=gathered.at[me * here + n],
+                src_ref=reduced.at[n, pl.ds(start, high - low), :],
+                dst_ref=gathered.at[me * here + n, pl.ds(low, high - low), :],
                 send_sem=send_1.at[j, n],
                 recv_sem=recv_1.at[j, n],
                 device_id={"frames": to * PLANE + spot},
             )
+
+        def each_1(j, n, to, act):
+            @pl.when(to == 0)
+            def _():
+                act(copy_1(j, n, REACH, plane_window))
+
+            @pl.when(to == planes - 1)
+            def _():
+                act(copy_1(j, n, 0, plane_window - REACH))
+
+            if planes > 2:
+
+                @pl.when((to > 0) & (to < planes - 1))
+                def _():
+                    act(copy_1(j, n, 0, plane_window))
 
         def copy_2(j, n):
             first = across // PAIR * PAIR
@@ -306,7 +331,7 @@
             if n == 0:
                 pl.semaphore_wait(barrier, parts - 1)
             for j in range(1, planes):
-                copy_1(j, n).start()
+                each_1(j, n, flip(plane, j), lambda copy: copy.start())
             copy_2(0, n).start()
             copy_3(0, n).start()
 
@@ -333,12 +358,27 @@
         )
         matrix[...] = jnp.where(same, wide, 0.0).astype(jnp.bfloat16)
 
-        def stack_one(t, block):
-            stacked[t] = (
+        def stack_one(place, block):
+            stacked[place] = (
                 jnp.dot(left[...], block, preferred_element_type=jnp.float32)
                 .astype(jnp.bfloat16)
                 .reshape(ORIENT * 2, rows, QUART)
             )
+
+        def coefficients(where):
+            for o in range(ORIENT):
+                value = jnp.dot(
+                    stacked[:, where, :, 2 * o].reshape(planes * here * rows, QUART),
+                    right[o, 0],
+                    preferred_element_type=jnp.float32,
+                ) + jnp.dot(
+                    stacked[:, where, :, 2 * o + 1].reshape(planes * here * rows, QUART),
+                    right[o, 1],
+                    preferred_element_type=jnp.float32,
+                )
+                value = value.astype(jnp.bfloat16).reshape(planes, here, rows, 2 * QUART)
+                for p in range(planes):
+                    coeffs[pl.ds((p * PLANE + where) * here, here), o] = value[p]
 
         own_rows = pl.ds(pl.multiple_of(spot * rows, rows), window)
 
@@ -346,7 +386,7 @@
             @pl.loop(0, here)
             def _(n):
                 t = frame_of(j, where, n)
-                stack_one(t, gathered[t, own_rows, :])
+                stack_one((flip(plane, j), where, n), gathered[t, own_rows, :])
 
         def second(j):
             for n in range(here):
@@ -355,39 +395,29 @@
             stack_arrived(j, across)
 
         for n in range(here):
-            stack_one(me * here + n, reduced[n, pl.ds(pl.multiple_of(me * rows, rows), window), :])
+            stack_one((plane, spot, n), reduced[n, pl.ds(pl.multiple_of(me * rows, rows), window), :])
         for j in range(1, planes):
             for n in range(here):
-                copy_1(j, n).wait_recv()
+                each_1(j, n, plane, lambda copy: copy.wait_recv())
                 copy_2(j, n).start()
                 copy_3(j, n).start()
             stack_arrived(j, spot)
             second(j - 1)
+        load_right.wait()
+        coefficients(spot)
+        second(planes - 1)
         for j in range(planes):
             for n in range(here):
                 copy_3(j, n).wait_recv()
             stack_arrived(j, sibling)
-        second(planes - 1)
+        coefficients(across)
+        coefficients(sibling)
+        last = flip(across, 1)
         for j in range(planes):
             for n in range(here):
                 copy_4(j, n).wait_recv()
-            stack_arrived(j, flip(across, 1))
-
-        load_right.wait()
-        step = frames // 4
-        for o in range(ORIENT):
-            for part in range(4):
-                where = slice(part * step, (part + 1) * step)
-                value = jnp.dot(
-                    stacked[where, 2 * o].reshape(step * rows, QUART),
-                    right[o, 0],
-                    preferred_element_type=jnp.float32,
-                ) + jnp.dot(
-                    stacked[where, 2 * o + 1].reshape(step * rows, QUART),
-                    right[o, 1],
-                    preferred_element_type=jnp.float32,
-                )
-                coeffs[where, o] = value.astype(jnp.bfloat16).reshape(step, rows, 2 * QUART)
+            stack_arrived(j, last)
+        coefficients(last)
 
         counts = [jnp.int32(0)] * NSEG
         for t in range(frames):
@@ -416,49 +446,68 @@
             phase[:, t] = signal.astype(jnp.bfloat16)
             denom[t] = jnp.sum(real * real + imag * imag, axis=0) + 1.0
 
-        for o in range(ORIENT):
-            filtered = (
-                jnp.dot(
-                    matrix[...],
-                    phase[o].reshape(total, QUART),
-                    preferred_element_type=jnp.float32,
-                )
-                .astype(jnp.bfloat16)
-                .astype(jnp.float32)
-                .reshape(frames, rows, QUART)
-            )
-            real = coeffs[:, o, :, :QUART].astype(jnp.float32)
-            imag = coeffs[:, o, :, QUART:].astype(jnp.float32)
-            term = (real * real + imag * imag) * filtered
-            if o == 0:
-                numer[...] = term
-            elif o < ORIENT - 1:
-                numer[...] += term
-            else:
-                moved[...] = ((numer[...] + term) / denom[...]).astype(jnp.bfloat16)
-
         here_rows = pl.ds(pl.multiple_of(me * rows, rows), rows)
 
         def return_copy(j):
             to = peer(j)
             return pltpu.make_async_remote_copy(
                 src_ref=moved.at[pl.ds(to * here, here)],
-                dst_ref=landed.at[:, here_rows, :],
+                dst_ref=out_hbm.at[:, here_rows, :],
                 send_sem=send_b.at[j],
                 recv_sem=recv_b.at[j],
                 device_id={"frames": to},
             )
 
-        @pl.loop(1, parts)
-        def _(j):
-            return_copy(j).start()
-
-        landed[:, here_rows, :] = moved[pl.ds(me * here, here)]
+        crowd = parts // 2
+        near = me // crowd
+
+        def filter_half(number):
+            span = pl.ds(number * (frames // 2), frames // 2)
+            long_span = pl.ds(pl.multiple_of(number * (total // 2), total // 2), total // 2)
+            for o in range(ORIENT):
+                filtered = (
+                    jnp.dot(
+                        matrix[long_span, :],
+                        phase[o].reshape(total, QUART),
+                        preferred_element_type=jnp.float32,
+                    )
+                    .astype(jnp.bfloat16)
+                    .astype(jnp.float32)
+                    .reshape(frames // 2, rows, QUART)
+                )
+                real = coeffs[span, o, :, :QUART].astype(jnp.float32)
+                imag = coeffs[span, o, :, QUART:].astype(jnp.float32)
+                term = (real * real + imag * imag) * filtered
+                if o == 0:
+                    numer[...] = term
+                elif o < ORIENT - 1:
+                    numer[...] += term
+                else:
+                    moved[span] = ((numer[...] + term) / denom[span]).astype(jnp.bfloat16)
+
+        filter_half(1 - near)
+
+        @pl.loop(0, crowd)
+        def _(k):
+            to = (1 - near) * crowd + lax.rem(me + k, crowd)
+            return_copy(lax.rem(to + parts - me, parts)).start()
+
+        filter_half(near)
+
+        @pl.loop(1, crowd)
+        def _(k):
+            to = near * crowd + lax.rem(me + k, crowd)
+            return_copy(lax.rem(to + parts - me, parts)).start()
+
+        store = pltpu.make_async_copy(
+            moved.at[pl.ds(me * here, here)], out_hbm.at[:, here_rows, :], store_sem
+        )
+        store.start()
 
         for n in range(here):
             for j in range(planes):
                 if j:
-                    copy_1(j, n).wait_send()
+                    each_1(j, n, flip(plane, j), lambda copy: copy.wait_send())
                 copy_2(j, n).wait_send()
                 copy_3(j, n).wait_send()
                 copy_4(j, n).wait_send()
@@ -466,10 +515,6 @@
         @pl.loop(1, parts)
         def _(j):
             return_copy(j).wait_recv()
-
-        out[...] = landed[...].astype(jnp.float32)
-        store = pltpu.make_async_copy(out, out_hbm, store_sem)
-        store.start()
 
         @pl.loop(1, parts)
         def _(j):
@@ -483,7 +528,7 @@
     smem = pl.BlockSpec(memory_space=pltpu.SMEM)
     return pl.pallas_call(
         kernel,
-        out_shape=jax.ShapeDtypeStruct((here, QUART, QUART), f32),
+        out_shape=jax.ShapeDtypeStruct((here, QUART, QUART), bf16),
         in_specs=[smem, smem, vmem, anywhere, anywhere, anywhere, vmem, anywhere],
         out_specs=anywhere,
         scratch_shapes=[
@@ -494,15 +539,13 @@
             pltpu.VMEM((here, IMG, QUART), bf16),
             pltpu.VMEM((here, QUART + 2 * REACH, QUART), bf16),
             pltpu.VMEM((frames, plane_window, QUART), bf16),
-            pltpu.VMEM((frames, ORIENT * 2, rows, QUART), bf16),
+            pltpu.VMEM((planes, PLANE, here, ORIENT * 2, rows, QUART), bf16),
             pltpu.VMEM((frames, ORIENT, rows, 2 * QUART), bf16),
             pltpu.VMEM((ORIENT, frames, rows, QUART), bf16),
             pltpu.VMEM((total, total), bf16),
-            pltpu.VMEM((frames, rows, QUART), f32),
+            pltpu.VMEM((frames // 2, rows, QUART), f32),
             pltpu.VMEM((frames, rows, QUART), f32),
             pltpu.VMEM((frames, rows, QUART), bf16),
-            pltpu.VMEM((here, QUART, QUART), bf16),
-            pltpu.VMEM((here, QUART, QUART), f32),
             dma((3 + here * chunks,)),
             dma,
             dma((planes, here)),
@@ -533,7 +576,7 @@
         jnp.asarray(np.ascontiguousarray(down.T)),
         jnp.asarray(left_window(rows)),
         jnp.asarray(right_tables()),
-    )
+    ).astype(jnp.float32)
 
 
 def solution(mesh):

time: 38.4 us -> 38 us (0.990); the launches traced: 38.2 us -> 37.4 us
  local copies, waits for them, and re-layouts: 1.87 us -> 0 us
  other arithmetic: 0 us -> 1.78 us
  Pallas kernels: 36.3 us -> 35.6 us
    unnamed x1 -> x0, local copies, waits for them, and re-layouts: 1.87 us -> none
    convert_element_type x0 -> x1, other arithmetic: none -> 1.78 us  [kernel_body(): return make_kernel(parts, here, rows)(segments, ref_pick, band_taps[None,...]
    pallas_call x1, Pallas kernels: 36.3 us -> 35.6 us  [kernel_body(): make_kernel(parts, here, rows)]
where the time goes in v3:
time: 38 us; the launch traced here: 37.4 us
  Pallas kernels  35.6 us (94%)
  other arithmetic  1.78 us (5%)
    pallas_call x1, Pallas kernels, kernel_body(): make_kernel(parts, here, rows)  35.6 us
    convert_element_type x1, other arithmetic, kernel_body(): return make_kernel(parts, here, rows)(segments, ref_pick, band_taps[None,...  1.78 us

profile of v3, /device:TPU:1, one launch (start us, length us, event | category | flops | bytes accessed | tf_op | source)
XLA Modules:
  0.0 37.4 jit_solution(6012786155983498646)
XLA Ops:
  0.0 35.6 %shard_map.82 = bf16[2,256,256]{2,1,0:T(8,128)(2,1)} custom-call(s32[32]{0:T(128)} %segments.1, s32[4]{0:T(128)} %picks.1, bf16[1,32]{1,0:T(2,128)(2,1)} %bitcast.1, bf16[2,1024,1024]{2,1,0:T(8,128)(2,1)} %video_hbm.1, bf16[256,1024]{1,0:T(8,128)(2,1)} %constant.8.clone.down_hbm, bf16[1024,256]{1,0:T(8,128)(2,1)} %constant.9.clone.down_t_hbm, ...), custom_call_target="tpu_custom_call" | custom-call | tf_op jit(solution)/shard_map/pallas_call | solution.py:570
  35.6 1.8 %convert_element_type.3 = f32[2,256,256]{2,1,0:T(8,128)} convert(bf16[2,256,256]{2,1,0:T(8,128)(2,1)} %shard_map.82) | non-fusion elementwise | flops 131072 | bytes 786432 | tf_op jit(solution)/shard_map/convert_element_type | solution.py:579

commit v4 on v3

--- a/solution.py
+++ b/solution.py
@@ -396,16 +396,17 @@
 
         for n in range(here):
             stack_one((plane, spot, n), reduced[n, pl.ds(pl.multiple_of(me * rows, rows), window), :])
-        for j in range(1, planes):
-            for n in range(here):
+        for n in range(here):
+            for j in range(1, planes):
                 each_1(j, n, plane, lambda copy: copy.wait_recv())
                 copy_2(j, n).start()
                 copy_3(j, n).start()
+        for j in range(1, planes):
             stack_arrived(j, spot)
-            second(j - 1)
         load_right.wait()
+        for j in range(planes):
+            second(j)
         coefficients(spot)
-        second(planes - 1)
         for j in range(planes):
             for n in range(here):
                 copy_3(j, n).wait_recv()

time: 38 us -> 37.4 us (0.984)
  Pallas kernels: 35.6 us -> 35 us
    pallas_call x1, Pallas kernels: 35.6 us -> 35 us  [kernel_body(): make_kernel(parts, here, rows)]
where the time goes in v4:
time: 37.4 us; the launch traced here: 36.8 us
  Pallas kernels  35 us (94%)
  other arithmetic  1.78 us (5%)
    pallas_call x1, Pallas kernels, kernel_body(): make_kernel(parts, here, rows)  35 us
    convert_element_type x1, other arithmetic, kernel_body(): return make_kernel(parts, here, rows)(segments, ref_pick, band_taps[None,...  1.78 us

profile of v4, /device:TPU:1, one launch (start us, length us, event | category | flops | bytes accessed | tf_op | source)
XLA Modules:
  0.0 36.8 jit_solution(10295035612098889874)
XLA Ops:
  0.0 35.0 %shard_map.82 = bf16[2,256,256]{2,1,0:T(8,128)(2,1)} custom-call(s32[32]{0:T(128)} %segments.1, s32[4]{0:T(128)} %picks.1, bf16[1,32]{1,0:T(2,128)(2,1)} %bitcast.1, bf16[2,1024,1024]{2,1,0:T(8,128)(2,1)} %video_hbm.1, bf16[256,1024]{1,0:T(8,128)(2,1)} %constant.8.clone.down_hbm, bf16[1024,256]{1,0:T(8,128)(2,1)} %constant.9.clone.down_t_hbm, ...), custom_call_target="tpu_custom_call" | custom-call | tf_op jit(solution)/shard_map/pallas_call | solution.py:571
  35.0 1.8 %convert_element_type.3 = f32[2,256,256]{2,1,0:T(8,128)} convert(bf16[2,256,256]{2,1,0:T(8,128)(2,1)} %shard_map.82) | non-fusion elementwise | flops 131072 | bytes 786432 | tf_op jit(solution)/shard_map/convert_element_type | solution.py:580
